TPU v7x, 32 devices: a whole 2x2x4 slice. The times are simulated.
32 devices in a mesh: ctx: 16 (over z, y, core), mp: 2 (over x).
Axes of the slice: x: 2, y: 2, z: 4, core: 2. Of those that a mesh axis runs over, the one named last changes fastest.
Arguments:
- features: bfloat16 [3, 8192, 4096], P(None, 'ctx', 'mp'), may hold values from -6 to 6
- short_filter: float32 [3, 7, 4096], P(None, None, 'mp'), may hold values from -2 to 2
- residues: float32 [4096, 16], P('mp'), may hold values from -1.5 to 1.5
- rates: float32 [4096, 16], P('mp'), as said below
- out_weight: bfloat16 [4096, 4096], P('ctx', 'mp'), may hold values from -0.125 to 0.125
Outputs:
- mixed: bfloat16 [8192, 4096], P('ctx', 'mp')
Inputs may be any that keep to these rules, and one draw needn't show every extreme that they name: `rates`: every rate lies between 0.3 / 8192 and 0.08.
All inputs are finite; a program needn't handle non-finite values.
Results may differ from a plain program's by a relative error of at most 0.0058.
Values may be sent and summed in bfloat16 or wider, within the bound.
A program may use at most 128 MiB of HBM per device.

v0:
```python
import jax
import jax.numpy as jnp
from jax import lax
from jax.sharding import PartitionSpec as P

BLOCK = 128


def shifted(block, axis, distance):
    devices = range(lax.axis_size(axis))
    route = [(i - distance, i) for i in devices if i - distance in devices]
    return lax.ppermute(block, axis, route)


def prefix(value, axis, join, neutral):
    count, mine = (lax.axis_size(axis), lax.axis_index(axis))
    pieces = jax.tree.map(lambda part: lax.all_gather(part, axis), value)
    subtotal = jax.tree.map(
        lambda part, zero: jnp.full_like(part, 0) + jnp.asarray(zero, part.dtype), value, neutral
    )

    def step(position, subtotal):
        longer = join(subtotal, jax.tree.map(lambda part: part[position], pieces))
        return jax.tree.map(lambda new, old: jnp.where(position < mine, new, old), longer, subtotal)

    return lax.fori_loop(0, count - 1, step, subtotal)


def short_conv(extended, taps, length):
    width = taps.shape[1]
    running = jnp.zeros((extended.shape[0], length, extended.shape[2]), jnp.float32)
    for offset in range(width):
        window = extended[:, width - 1 - offset : width - 1 - offset + length, :].astype(
            jnp.float32
        )
        running = running + taps[:, offset, None, :] * window
    return running


def block_toeplitz(sub_rows, scaled, rates, positions):
    pieces, span, channels = sub_rows.shape
    block_width = 128
    groups = channels // block_width
    lag_table = (
        jnp.arange(span, dtype=jnp.int32)[:, None] - jnp.arange(span, dtype=jnp.int32)[None, :]
    )
    causal = lag_table >= 0

    def one_group(packed):
        group_scaled, group_rates, group_rows = packed
        ahead = group_scaled[:, :, None] * jnp.exp(
            -group_rates[:, :, None] * positions[None, None, :]
        )
        behind = jnp.exp(group_rates[:, :, None] * positions[None, None, :])
        tile = jnp.einsum("cni,cnj->cij", ahead, behind, precision=lax.Precision.HIGHEST)
        tile = jnp.where(causal[None], tile, jnp.float32(0.0))
        return jnp.einsum(
            "cij,bjc->bic", tile, group_rows.astype(jnp.float32), precision=lax.Precision.HIGHEST
        )

    modes = scaled.shape[1]
    grouped_rows = jnp.moveaxis(sub_rows.reshape(pieces, span, groups, block_width), 2, 0)
    outputs = lax.map(
        one_group,
        (
            scaled.reshape(groups, block_width, modes),
            rates.reshape(groups, block_width, modes),
            grouped_rows,
        ),
    )
    return jnp.moveaxis(outputs, 0, 2).reshape(pieces, span, channels)


def chain_combine(earlier, later):
    return (earlier[0] * later[0], earlier[1] * later[0] + later[1])


def body(features, short_filter, residues, rates, out_weight):
    length = features.shape[1]
    channels = features.shape[2]
    width = short_filter.shape[1]
    before = shifted(features[:, length - (width - 1) :, :], "ctx", 1)
    extended = jnp.concatenate([before, features], axis=1)
    featured = short_conv(extended, short_filter, length)
    gated = (featured[1] * featured[2]).astype(jnp.bfloat16)
    scaled = residues * jnp.sqrt(-jnp.expm1(-2.0 * rates))
    span = BLOCK
    pieces = length // span
    positions = jnp.arange(span, dtype=jnp.float32)
    sub_rows = gated.reshape(pieces, span, channels)
    local = block_toeplitz(sub_rows, scaled, rates, positions)
    end_weights = jnp.exp(-rates[None] * (span - positions)[:, None, None])
    start_weights = jnp.exp(-rates[None] * positions[:, None, None]) * scaled[None]
    sub_states = jnp.einsum(
        "bjc,jcn->bcn", sub_rows.astype(jnp.float32), end_weights, precision=lax.Precision.HIGHEST
    )
    step_decay = jnp.exp(-rates * span)

    def advance(carried, state):
        return (step_decay * carried + state, carried)

    own_state, prefixes = lax.scan(advance, jnp.zeros_like(step_decay), sub_states)
    block_decay = jnp.exp(-rates * length)
    identity = (jnp.ones_like(block_decay), jnp.zeros_like(own_state))
    _, carried = prefix((block_decay, own_state), "ctx", chain_combine, identity)
    piece_offsets = span * jnp.arange(pieces, dtype=jnp.float32)
    powers = jnp.exp(-rates[None] * piece_offsets[:, None, None])
    carried_all = prefixes + powers * carried[None]
    far_term = jnp.einsum(
        "icn,bcn->bic", start_weights, carried_all, precision=lax.Precision.HIGHEST
    )
    long_rows = (local + far_term).reshape(length, channels)
    combined = (featured[0] * long_rows).astype(jnp.bfloat16)
    gathered = lax.all_gather(combined, "mp", axis=1, tiled=True)
    result = jnp.dot(
        gathered,
        lax.all_gather(out_weight, "ctx", axis=0, tiled=True),
        preferred_element_type=jnp.float32,
    )
    return result.astype(jnp.bfloat16)


def solution(mesh):
    placed = (
        P(None, "ctx", "mp"),
        P(None, None, "mp"),
        P("mp", None),
        P("mp", None),
        P("ctx", "mp"),
    )
    return jax.shard_map(
        body, mesh=mesh, in_specs=placed, out_specs=P("ctx", "mp"), check_vma=False
    )
```

profile of v0, /device:TPU:0, one launch (start us, length us, event | category | flops | bytes accessed | tf_op | source)
XLA Modules:
  0.0 717.9 jit_solution(18163062888685252601)
XLA Ops:
  17.7 19.1 %multiply_add_fusion = f32[3,512,2048]{2,1,0:T(8,128)S(1)} fusion(bf16[3,512,2048]{2,1,0:T(8,128)(2,1)} %param.11, bf16[3,6,2048]{2,1,0:T(8,128)(2,1)S(1)} %collective-permute-done, f32[3,2048]{1,0:T(4,128)S(1)} %get-tuple-element.303, f32[3,2048]{1,0:T(4,128)S(1)} %get-tuple-element.304, f32[3,2048]{1,0:T(4,128)S(1)} %get-tuple-element.305, ...), kind=kLoop, calls=%fused_computation.46 | loop fusion | flops 119537664 | bytes 19120128 | tf_op jit(solution)/shard_map/add | solution.py:36
  36.8 4.5 copy-done
  44.5 17.5 %fusion.50 = f32[4,2048,16]{2,0,1:T(4,128)} fusion(bf16[4,128,2048]{1,0,2:T(4,128)(2,1)} %copy.20, f32[128]{0:T(128)S(1)} %iota_subtract_fusion, f32[2048,16]{1,0:T(8,128)} %copy.19), kind=kOutput, calls=%fused_computation.67 | convolution fusion | flops 205520896 | bytes 2753024 | tf_op jit(solution)/shard_map/bjc,jcn->bcn/dot_general | solution.py:94
  63.5 2.9 copy.27
  66.4 3.4 copy.21
  71.0 368.5 %while.39 = (s32[]{:T(128)}, f32[16,4,128,128]{2,1,3,0:T(4,128)}, bf16[16,4,128,128]{2,1,3,0:T(4,128)(2,1)}, f32[16,128,16]{1,0,2:T(8,128)S(1)}, f32[16,128,16]{1,0,2:T(8,128)S(1)}, /*index=5*/s32[]{:T(128)}) while((s32[]{:T(128)}, f32[16,4,128,128]{2,1,3,0:T(4,128)}, bf16[16,4,128,128]{2,1,3,0:T(4,128)(2,1)}, ...), condition=%wide.region_1.2_spmd.clone.clone, body=%wide.region_0.1_spmd.clone.clone.sunk | while | flops 506234880 | bytes 17327184 | solution.py:63
  71.6 14.0 %fusion.72 = f32[128,128,128]{2,1,0:T(8,128)S(1)} fusion(f32[128,16]{1,0:T(8,128)S(1)} %copy.68, f32[128,16]{1,0:T(8,128)S(1)} %copy.69, f32[128,16]{1,0:T(8,128)S(1)} %copy.70), kind=kOutput, calls=%fused_computation.12.clone.1 | convolution fusion | flops 403439616 | bytes 8413184 | tf_op jit(solution)/shard_map/while/body/eval_jaxpr/cni,cnj->cij/dot_general | solution.py:55
  85.6 8.2 %fusion.73 = f32[16,4,128,128]{2,1,3,0:T(4,128)} fusion(f32[16,4,128,128]{2,1,3,0:T(4,128)} %get-tuple-element.417, s32[]{:T(128)S(6)} %copy.77, f32[128,128,128]{2,1,0:T(8,128)S(1)} %fusion.72, pred[128,128]{1,0:T(8,128)(4,1)S(1)} %subtract_compare_fusion.2, bf16[16,4,128,128]{2,1,3,0:T(4,128)(2,1)} %get-tuple-element.424), kind=kOutput, calls=%fused_computation.9.clone.1 | convolution fusion | flops 102760448 | bytes 8799232 | tf_op jit(solution)/shard_map/while/body/eval_jaxpr/cij,bjc->bic/dot_general | solution.py:57
  94.2 14.0 %fusion.72 = f32[128,128,128]{2,1,0:T(8,128)S(1)} fusion(f32[128,16]{1,0:T(8,128)S(1)} %copy.68, f32[128,16]{1,0:T(8,128)S(1)} %copy.69, f32[128,16]{1,0:T(8,128)S(1)} %copy.70), kind=kOutput, calls=%fused_computation.12.clone.1 | convolution fusion | flops 403439616 | bytes 8413184 | tf_op jit(solution)/shard_map/while/body/eval_jaxpr/cni,cnj->cij/dot_general | solution.py:55
  108.2 8.2 %fusion.73 = f32[16,4,128,128]{2,1,3,0:T(4,128)} fusion(f32[16,4,128,128]{2,1,3,0:T(4,128)} %get-tuple-element.417, s32[]{:T(128)S(6)} %copy.77, f32[128,128,128]{2,1,0:T(8,128)S(1)} %fusion.72, pred[128,128]{1,0:T(8,128)(4,1)S(1)} %subtract_compare_fusion.2, bf16[16,4,128,128]{2,1,3,0:T(4,128)(2,1)} %get-tuple-element.424), kind=kOutput, calls=%fused_computation.9.clone.1 | convolution fusion | flops 102760448 | bytes 8799232 | tf_op jit(solution)/shard_map/while/body/eval_jaxpr/cij,bjc->bic/dot_general | solution.py:57
  116.8 14.0 %fusion.72 = f32[128,128,128]{2,1,0:T(8,128)S(1)} fusion(f32[128,16]{1,0:T(8,128)S(1)} %copy.68, f32[128,16]{1,0:T(8,128)S(1)} %copy.69, f32[128,16]{1,0:T(8,128)S(1)} %copy.70), kind=kOutput, calls=%fused_computation.12.clone.1 | convolution fusion | flops 403439616 | bytes 8413184 | tf_op jit(solution)/shard_map/while/body/eval_jaxpr/cni,cnj->cij/dot_general | solution.py:55
  130.9 8.2 %fusion.73 = f32[16,4,128,128]{2,1,3,0:T(4,128)} fusion(f32[16,4,128,128]{2,1,3,0:T(4,128)} %get-tuple-element.417, s32[]{:T(128)S(6)} %copy.77, f32[128,128,128]{2,1,0:T(8,128)S(1)} %fusion.72, pred[128,128]{1,0:T(8,128)(4,1)S(1)} %subtract_compare_fusion.2, bf16[16,4,128,128]{2,1,3,0:T(4,128)(2,1)} %get-tuple-element.424), kind=kOutput, calls=%fused_computation.9.clone.1 | convolution fusion | flops 102760448 | bytes 8799232 | tf_op jit(solution)/shard_map/while/body/eval_jaxpr/cij,bjc->bic/dot_general | solution.py:57
  139.4 14.0 %fusion.72 = f32[128,128,128]{2,1,0:T(8,128)S(1)} fusion(f32[128,16]{1,0:T(8,128)S(1)} %copy.68, f32[128,16]{1,0:T(8,128)S(1)} %copy.69, f32[128,16]{1,0:T(8,128)S(1)} %copy.70), kind=kOutput, calls=%fused_computation.12.clone.1 | convolution fusion | flops 403439616 | bytes 8413184 | tf_op jit(solution)/shard_map/while/body/eval_jaxpr/cni,cnj->cij/dot_general | solution.py:55
  153.4 8.2 %fusion.73 = f32[16,4,128,128]{2,1,3,0:T(4,128)} fusion(f32[16,4,128,128]{2,1,3,0:T(4,128)} %get-tuple-element.417, s32[]{:T(128)S(6)} %copy.77, f32[128,128,128]{2,1,0:T(8,128)S(1)} %fusion.72, pred[128,128]{1,0:T(8,128)(4,1)S(1)} %subtract_compare_fusion.2, bf16[16,4,128,128]{2,1,3,0:T(4,128)(2,1)} %get-tuple-element.424), kind=kOutput, calls=%fused_computation.9.clone.1 | convolution fusion | flops 102760448 | bytes 8799232 | tf_op jit(solution)/shard_map/while/body/eval_jaxpr/cij,bjc->bic/dot_general | solution.py:57
  162.0 14.0 %fusion.72 = f32[128,128,128]{2,1,0:T(8,128)S(1)} fusion(f32[128,16]{1,0:T(8,128)S(1)} %copy.68, f32[128,16]{1,0:T(8,128)S(1)} %copy.69, f32[128,16]{1,0:T(8,128)S(1)} %copy.70), kind=kOutput, calls=%fused_computation.12.clone.1 | convolution fusion | flops 403439616 | bytes 8413184 | tf_op jit(solution)/shard_map/while/body/eval_jaxpr/cni,cnj->cij/dot_general | solution.py:55
  176.0 8.2 %fusion.73 = f32[16,4,128,128]{2,1,3,0:T(4,128)} fusion(f32[16,4,128,128]{2,1,3,0:T(4,128)} %get-tuple-element.417, s32[]{:T(128)S(6)} %copy.77, f32[128,128,128]{2,1,0:T(8,128)S(1)} %fusion.72, pred[128,128]{1,0:T(8,128)(4,1)S(1)} %subtract_compare_fusion.2, bf16[16,4,128,128]{2,1,3,0:T(4,128)(2,1)} %get-tuple-element.424), kind=kOutput, calls=%fused_computation.9.clone.1 | convolution fusion | flops 102760448 | bytes 8799232 | tf_op jit(solution)/shard_map/while/body/eval_jaxpr/cij,bjc->bic/dot_general | solution.py:57
  184.6 14.0 %fusion.72 = f32[128,128,128]{2,1,0:T(8,128)S(1)} fusion(f32[128,16]{1,0:T(8,128)S(1)} %copy.68, f32[128,16]{1,0:T(8,128)S(1)} %copy.69, f32[128,16]{1,0:T(8,128)S(1)} %copy.70), kind=kOutput, calls=%fused_computation.12.clone.1 | convolution fusion | flops 403439616 | bytes 8413184 | tf_op jit(solution)/shard_map/while/body/eval_jaxpr/cni,cnj->cij/dot_general | solution.py:55
  198.6 8.2 %fusion.73 = f32[16,4,128,128]{2,1,3,0:T(4,128)} fusion(f32[16,4,128,128]{2,1,3,0:T(4,128)} %get-tuple-element.417, s32[]{:T(128)S(6)} %copy.77, f32[128,128,128]{2,1,0:T(8,128)S(1)} %fusion.72, pred[128,128]{1,0:T(8,128)(4,1)S(1)} %subtract_compare_fusion.2, bf16[16,4,128,128]{2,1,3,0:T(4,128)(2,1)} %get-tuple-element.424), kind=kOutput, calls=%fused_computation.9.clone.1 | convolution fusion | flops 102760448 | bytes 8799232 | tf_op jit(solution)/shard_map/while/body/eval_jaxpr/cij,bjc->bic/dot_general | solution.py:57
  207.2 14.0 %fusion.72 = f32[128,128,128]{2,1,0:T(8,128)S(1)} fusion(f32[128,16]{1,0:T(8,128)S(1)} %copy.68, f32[128,16]{1,0:T(8,128)S(1)} %copy.69, f32[128,16]{1,0:T(8,128)S(1)} %copy.70), kind=kOutput, calls=%fused_computation.12.clone.1 | convolution fusion | flops 403439616 | bytes 8413184 | tf_op jit(solution)/shard_map/while/body/eval_jaxpr/cni,cnj->cij/dot_general | solution.py:55
  221.2 8.2 %fusion.73 = f32[16,4,128,128]{2,1,3,0:T(4,128)} fusion(f32[16,4,128,128]{2,1,3,0:T(4,128)} %get-tuple-element.417, s32[]{:T(128)S(6)} %copy.77, f32[128,128,128]{2,1,0:T(8,128)S(1)} %fusion.72, pred[128,128]{1,0:T(8,128)(4,1)S(1)} %subtract_compare_fusion.2, bf16[16,4,128,128]{2,1,3,0:T(4,128)(2,1)} %get-tuple-element.424), kind=kOutput, calls=%fused_computation.9.clone.1 | convolution fusion | flops 102760448 | bytes 8799232 | tf_op jit(solution)/shard_map/while/body/eval_jaxpr/cij,bjc->bic/dot_general | solution.py:57
  229.7 14.0 %fusion.72 = f32[128,128,128]{2,1,0:T(8,128)S(1)} fusion(f32[128,16]{1,0:T(8,128)S(1)} %copy.68, f32[128,16]{1,0:T(8,128)S(1)} %copy.69, f32[128,16]{1,0:T(8,128)S(1)} %copy.70), kind=kOutput, calls=%fused_computation.12.clone.1 | convolution fusion | flops 403439616 | bytes 8413184 | tf_op jit(solution)/shard_map/while/body/eval_jaxpr/cni,cnj->cij/dot_general | solution.py:55
  243.8 8.2 %fusion.73 = f32[16,4,128,128]{2,1,3,0:T(4,128)} fusion(f32[16,4,128,128]{2,1,3,0:T(4,128)} %get-tuple-element.417, s32[]{:T(128)S(6)} %copy.77, f32[128,128,128]{2,1,0:T(8,128)S(1)} %fusion.72, pred[128,128]{1,0:T(8,128)(4,1)S(1)} %subtract_compare_fusion.2, bf16[16,4,128,128]{2,1,3,0:T(4,128)(2,1)} %get-tuple-element.424), kind=kOutput, calls=%fused_computation.9.clone.1 | convolution fusion | flops 102760448 | bytes 8799232 | tf_op jit(solution)/shard_map/while/body/eval_jaxpr/cij,bjc->bic/dot_general | solution.py:57
  252.3 14.0 %fusion.72 = f32[128,128,128]{2,1,0:T(8,128)S(1)} fusion(f32[128,16]{1,0:T(8,128)S(1)} %copy.68, f32[128,16]{1,0:T(8,128)S(1)} %copy.69, f32[128,16]{1,0:T(8,128)S(1)} %copy.70), kind=kOutput, calls=%fused_computation.12.clone.1 | convolution fusion | flops 403439616 | bytes 8413184 | tf_op jit(solution)/shard_map/while/body/eval_jaxpr/cni,cnj->cij/dot_general | solution.py:55
  266.4 8.2 %fusion.73 = f32[16,4,128,128]{2,1,3,0:T(4,128)} fusion(f32[16,4,128,128]{2,1,3,0:T(4,128)} %get-tuple-element.417, s32[]{:T(128)S(6)} %copy.77, f32[128,128,128]{2,1,0:T(8,128)S(1)} %fusion.72, pred[128,128]{1,0:T(8,128)(4,1)S(1)} %subtract_compare_fusion.2, bf16[16,4,128,128]{2,1,3,0:T(4,128)(2,1)} %get-tuple-element.424), kind=kOutput, calls=%fused_computation.9.clone.1 | convolution fusion | flops 102760448 | bytes 8799232 | tf_op jit(solution)/shard_map/while/body/eval_jaxpr/cij,bjc->bic/dot_general | solution.py:57
  274.9 14.0 %fusion.72 = f32[128,128,128]{2,1,0:T(8,128)S(1)} fusion(f32[128,16]{1,0:T(8,128)S(1)} %copy.68, f32[128,16]{1,0:T(8,128)S(1)} %copy.69, f32[128,16]{1,0:T(8,128)S(1)} %copy.70), kind=kOutput, calls=%fused_computation.12.clone.1 | convolution fusion | flops 403439616 | bytes 8413184 | tf_op jit(solution)/shard_map/while/body/eval_jaxpr/cni,cnj->cij/dot_general | solution.py:55
  289.0 8.2 %fusion.73 = f32[16,4,128,128]{2,1,3,0:T(4,128)} fusion(f32[16,4,128,128]{2,1,3,0:T(4,128)} %get-tuple-element.417, s32[]{:T(128)S(6)} %copy.77, f32[128,128,128]{2,1,0:T(8,128)S(1)} %fusion.72, pred[128,128]{1,0:T(8,128)(4,1)S(1)} %subtract_compare_fusion.2, bf16[16,4,128,128]{2,1,3,0:T(4,128)(2,1)} %get-tuple-element.424), kind=kOutput, calls=%fused_computation.9.clone.1 | convolution fusion | flops 102760448 | bytes 8799232 | tf_op jit(solution)/shard_map/while/body/eval_jaxpr/cij,bjc->bic/dot_general | solution.py:57
  297.5 14.0 %fusion.72 = f32[128,128,128]{2,1,0:T(8,128)S(1)} fusion(f32[128,16]{1,0:T(8,128)S(1)} %copy.68, f32[128,16]{1,0:T(8,128)S(1)} %copy.69, f32[128,16]{1,0:T(8,128)S(1)} %copy.70), kind=kOutput, calls=%fused_computation.12.clone.1 | convolution fusion | flops 403439616 | bytes 8413184 | tf_op jit(solution)/shard_map/while/body/eval_jaxpr/cni,cnj->cij/dot_general | solution.py:55
  311.6 8.2 %fusion.73 = f32[16,4,128,128]{2,1,3,0:T(4,128)} fusion(f32[16,4,128,128]{2,1,3,0:T(4,128)} %get-tuple-element.417, s32[]{:T(128)S(6)} %copy.77, f32[128,128,128]{2,1,0:T(8,128)S(1)} %fusion.72, pred[128,128]{1,0:T(8,128)(4,1)S(1)} %subtract_compare_fusion.2, bf16[16,4,128,128]{2,1,3,0:T(4,128)(2,1)} %get-tuple-element.424), kind=kOutput, calls=%fused_computation.9.clone.1 | convolution fusion | flops 102760448 | bytes 8799232 | tf_op jit(solution)/shard_map/while/body/eval_jaxpr/cij,bjc->bic/dot_general | solution.py:57
  320.1 14.0 %fusion.72 = f32[128,128,128]{2,1,0:T(8,128)S(1)} fusion(f32[128,16]{1,0:T(8,128)S(1)} %copy.68, f32[128,16]{1,0:T(8,128)S(1)} %copy.69, f32[128,16]{1,0:T(8,128)S(1)} %copy.70), kind=kOutput, calls=%fused_computation.12.clone.1 | convolution fusion | flops 403439616 | bytes 8413184 | tf_op jit(solution)/shard_map/while/body/eval_jaxpr/cni,cnj->cij/dot_general | solution.py:55
  334.1 8.2 %fusion.73 = f32[16,4,128,128]{2,1,3,0:T(4,128)} fusion(f32[16,4,128,128]{2,1,3,0:T(4,128)} %get-tuple-element.417, s32[]{:T(128)S(6)} %copy.77, f32[128,128,128]{2,1,0:T(8,128)S(1)} %fusion.72, pred[128,128]{1,0:T(8,128)(4,1)S(1)} %subtract_compare_fusion.2, bf16[16,4,128,128]{2,1,3,0:T(4,128)(2,1)} %get-tuple-element.424), kind=kOutput, calls=%fused_computation.9.clone.1 | convolution fusion | flops 102760448 | bytes 8799232 | tf_op jit(solution)/shard_map/while/body/eval_jaxpr/cij,bjc->bic/dot_general | solution.py:57
  342.7 14.0 %fusion.72 = f32[128,128,128]{2,1,0:T(8,128)S(1)} fusion(f32[128,16]{1,0:T(8,128)S(1)} %copy.68, f32[128,16]{1,0:T(8,128)S(1)} %copy.69, f32[128,16]{1,0:T(8,128)S(1)} %copy.70), kind=kOutput, calls=%fused_computation.12.clone.1 | convolution fusion | flops 403439616 | bytes 8413184 | tf_op jit(solution)/shard_map/while/body/eval_jaxpr/cni,cnj->cij/dot_general | solution.py:55
  356.7 8.2 %fusion.73 = f32[16,4,128,128]{2,1,3,0:T(4,128)} fusion(f32[16,4,128,128]{2,1,3,0:T(4,128)} %get-tuple-element.417, s32[]{:T(128)S(6)} %copy.77, f32[128,128,128]{2,1,0:T(8,128)S(1)} %fusion.72, pred[128,128]{1,0:T(8,128)(4,1)S(1)} %subtract_compare_fusion.2, bf16[16,4,128,128]{2,1,3,0:T(4,128)(2,1)} %get-tuple-element.424), kind=kOutput, calls=%fused_computation.9.clone.1 | convolution fusion | flops 102760448 | bytes 8799232 | tf_op jit(solution)/shard_map/while/body/eval_jaxpr/cij,bjc->bic/dot_general | solution.py:57
  365.3 14.0 %fusion.72 = f32[128,128,128]{2,1,0:T(8,128)S(1)} fusion(f32[128,16]{1,0:T(8,128)S(1)} %copy.68, f32[128,16]{1,0:T(8,128)S(1)} %copy.69, f32[128,16]{1,0:T(8,128)S(1)} %copy.70), kind=kOutput, calls=%fused_computation.12.clone.1 | convolution fusion | flops 403439616 | bytes 8413184 | tf_op jit(solution)/shard_map/while/body/eval_jaxpr/cni,cnj->cij/dot_general | solution.py:55
  379.3 8.2 %fusion.73 = f32[16,4,128,128]{2,1,3,0:T(4,128)} fusion(f32[16,4,128,128]{2,1,3,0:T(4,128)} %get-tuple-element.417, s32[]{:T(128)S(6)} %copy.77, f32[128,128,128]{2,1,0:T(8,128)S(1)} %fusion.72, pred[128,128]{1,0:T(8,128)(4,1)S(1)} %subtract_compare_fusion.2, bf16[16,4,128,128]{2,1,3,0:T(4,128)(2,1)} %get-tuple-element.424), kind=kOutput, calls=%fused_computation.9.clone.1 | convolution fusion | flops 102760448 | bytes 8799232 | tf_op jit(solution)/shard_map/while/body/eval_jaxpr/cij,bjc->bic/dot_general | solution.py:57
  387.8 14.0 %fusion.72 = f32[128,128,128]{2,1,0:T(8,128)S(1)} fusion(f32[128,16]{1,0:T(8,128)S(1)} %copy.68, f32[128,16]{1,0:T(8,128)S(1)} %copy.69, f32[128,16]{1,0:T(8,128)S(1)} %copy.70), kind=kOutput, calls=%fused_computation.12.clone.1 | convolution fusion | flops 403439616 | bytes 8413184 | tf_op jit(solution)/shard_map/while/body/eval_jaxpr/cni,cnj->cij/dot_general | solution.py:55
  401.9 8.2 %fusion.73 = f32[16,4,128,128]{2,1,3,0:T(4,128)} fusion(f32[16,4,128,128]{2,1,3,0:T(4,128)} %get-tuple-element.417, s32[]{:T(128)S(6)} %copy.77, f32[128,128,128]{2,1,0:T(8,128)S(1)} %fusion.72, pred[128,128]{1,0:T(8,128)(4,1)S(1)} %subtract_compare_fusion.2, bf16[16,4,128,128]{2,1,3,0:T(4,128)(2,1)} %get-tuple-element.424), kind=kOutput, calls=%fused_computation.9.clone.1 | convolution fusion | flops 102760448 | bytes 8799232 | tf_op jit(solution)/shard_map/while/body/eval_jaxpr/cij,bjc->bic/dot_general | solution.py:57
  410.4 14.0 %fusion.72 = f32[128,128,128]{2,1,0:T(8,128)S(1)} fusion(f32[128,16]{1,0:T(8,128)S(1)} %copy.68, f32[128,16]{1,0:T(8,128)S(1)} %copy.69, f32[128,16]{1,0:T(8,128)S(1)} %copy.70), kind=kOutput, calls=%fused_computation.12.clone.1 | convolution fusion | flops 403439616 | bytes 8413184 | tf_op jit(solution)/shard_map/while/body/eval_jaxpr/cni,cnj->cij/dot_general | solution.py:55
  424.5 8.2 %fusion.73 = f32[16,4,128,128]{2,1,3,0:T(4,128)} fusion(f32[16,4,128,128]{2,1,3,0:T(4,128)} %get-tuple-element.417, s32[]{:T(128)S(6)} %copy.77, f32[128,128,128]{2,1,0:T(8,128)S(1)} %fusion.72, pred[128,128]{1,0:T(8,128)(4,1)S(1)} %subtract_compare_fusion.2, bf16[16,4,128,128]{2,1,3,0:T(4,128)(2,1)} %get-tuple-element.424), kind=kOutput, calls=%fused_computation.9.clone.1 | convolution fusion | flops 102760448 | bytes 8799232 | tf_op jit(solution)/shard_map/while/body/eval_jaxpr/cij,bjc->bic/dot_general | solution.py:57
  439.6 2.8 copy.43
  442.4 4.1 copy.44
  446.5 23.2 %while.41 = (s32[]{:T(128)}, f32[2048,16]{0,1:T(8,128)S(1)}, s32[]{:T(128)}, f32[16,2048,16]{1,0,2:T(8,128)S(1)}, f32[16,2048,16]{1,0,2:T(8,128)}, /*index=5*/s32[]{:T(128)}, s32[]{:T(128)}) while((s32[]{:T(128)}, f32[2048,16]{0,1:T(8,128)S(1)}, s32[]{:T(128)}, f32[16,2048,16]{1,0,2:T(8,128)S(1)}, f32[16,2048,16]{1,0,2:T(8,128)}, ...), condition=%wide.region_5.6_spmd.clone, body=%wide.region_4.5_spmd.clone.sunk | while | flops 131076 | bytes 1048685 | solution.py:26
  469.9 3.1 copy.25
  473.1 25.0 %bitcast_add_fusion.1 = f32[4,128,2048]{1,0,2:T(4,128)} fusion(f32[16,4,128,128]{2,1,3,0:T(4,128)} %get-tuple-element.167, f32[4,2048,16]{2,0,1:T(4,128)} %copy.25, f32[2048,16]{1,0:T(8,128)} %copy.24, f32[2048,16]{1,0:T(8,128)} %copy.19), kind=kOutput, calls=%fused_computation.65 | convolution fusion | flops 210763776 | bytes 9175040 | tf_op jit(solution)/shard_map/icn,bcn->bic/dot_general | solution.py:109
  498.0 5.3 copy.28
  503.3 5.4 fusion.49
  509.3 58.9 %all-gather.7.cloned.1.call-done = bf16[512,4096]{1,0:T(8,128)(2,1)} async-done(((bf16[512,2048]{1,0:T(8,128)(2,1)}), bf16[512,4096]{1,0:T(8,128)(2,1)}) %all-gather.7.cloned.1.call-update) | async-done | bytes 4194320 | tf_op jit(solution)/shard_map/all_gather | solution.py:114
  568.2 128.5 %all-gather.9.cloned.1.call-done = bf16[4096,2048]{1,0:T(8,128)(2,1)} async-done(((bf16[256,2048]{1,0:T(8,128)(2,1)}), bf16[4096,2048]{1,0:T(8,128)(2,1)}) %all-gather.9.cloned.1.call-update) | async-done | bytes 16777232 | tf_op jit(solution)/shard_map/all_gather | solution.py:117
  696.7 14.5 %convolution_convert_fusion = bf16[512,2048]{1,0:T(8,128)(2,1)} fusion(bf16[512,4096]{1,0:T(8,128)(2,1)} %all-gather.7.cloned.1.call-done, bf16[4096,2048]{1,0:T(8,128)(2,1)} %all-gather.9.cloned.1.call-done), kind=kOutput, calls=%fused_computation.66 | convolution fusion | flops 8590983168 | bytes 23068672 | tf_op jit(solution)/shard_map/dot_general | solution.py:115
  (174 shorter events, 46.0 us)
Async XLA Ops:
  6.5 433.0 %all-gather.11.cloned.1.call-start = ((), (), s32[]{:S(2)}) async-start(), calls=%async_computation.2 | async-start | bytes 2228224 | tf_op jit(solution)/shard_map/all_gather | solution.py:17
  7.5 10.2 %collective-permute-start = (bf16[3,6,2048]{2,1,0:T(8,128)(2,1)S(1)}, bf16[3,6,2048]{2,1,0:T(8,128)(2,1)S(1)}, u32[]{:S(2)}, u32[]{:S(2)}) collective-permute-start(bf16[3,6,2048]{2,1,0:T(8,128)(2,1)S(1)} %slice.53), channel_id=1, source_target_pairs={{0,2},{2,4},{4,6},{6,8},{8,10},{10,12},{12,14},{14,16},{16,18},{18... | collective-permute-start | bytes 221192 | tf_op jit(solution)/shard_map/ppermute | solution.py:12
  11.6 430.8 %all-gather.13.cloned.1.call-start = ((), (), s32[]{:S(2)}) async-start(), calls=%async_computation.3 | async-start | bytes 2228224 | tf_op jit(solution)/shard_map/all_gather | solution.py:17
  36.8 4.5 copy-start
  44.4 17.5 %copy-start.1 = (f32[3,512,2048]{2,1,0:T(8,128)S(1)}, f32[3,512,2048]{2,1,0:T(8,128)}, u32[]{:S(2)}) copy-start(f32[3,512,2048]{2,1,0:T(8,128)} %copy-done) | copy-start | bytes 37748740
  70.3 0.7 copy-start.2
  71.0 497.2 %all-gather.7.cloned.1.call-start = ((), (), s32[]{:S(2)}) async-start(), calls=%async_computation | async-start | bytes 6291456 | tf_op jit(solution)/shard_map/all_gather | solution.py:114
  508.8 187.9 %all-gather.9.cloned.1.call-start = ((), (), s32[]{:S(2)}) async-start(), calls=%async_computation.1 | async-start | bytes 17825792 | tf_op jit(solution)/shard_map/all_gather | solution.py:117
Sparse Core Ops, SparseCore 0:
  11.7 44.0 all-gather.10
  71.1 44.0 all-gather.12
  508.9 59.2 all-gather.6
  570.2 126.4 all-gather.8
where the time goes:
time: 729 us; the launch traced here: 718 us
  matrix products  413 us (57%)
  waiting for transfers between devices  188 us (26%)
  local copies, waits for them, and re-layouts  63.2 us (9%)
  other arithmetic  30 us (4%)
  between operations  13.5 us (2%)
  loops' own time  8 us (1%)
    dot_general x16, matrix products, one_group(): jnp.einsum('cni,cnj->cij', ahead, behind, precision=lax.Precision.HIGHEST)  224 us
    dot_general x16, matrix products, one_group(): jnp.einsum('cij,bjc->bic', tile, group_rows.astype(jnp.float32), precisio...  132 us
    all_gather x1, waiting for transfers between devices, body(): lax.all_gather(out_weight, 'ctx', axis=0, tiled=True)  128 us
    all_gather x1, waiting for transfers between devices, body(): gathered = lax.all_gather(combined, 'mp', axis=1, tiled=True)  58.9 us
    dot_general x1, matrix products, body(): jnp.einsum('icn,bcn->bic', start_weights, carried_all, precision=lax.Prec...  25 us
    dynamic_slice x15, local copies, waits for them, and re-layouts, step(): longer = join(subtotal, jax.tree.map(lambda part: part[position], pieces))  21.3 us
    add x1, other arithmetic, short_conv(): running = running + taps[:, offset, None, :] * window  19.1 us
    dot_general x1, matrix products, body(): jnp.einsum('bjc,jcn->bcn', sub_rows.astype(jnp.float32), end_weights, pre...  17.5 us
  transfers between devices with their start and end apart: 5, of which 2 were waited for; matrix products, arithmetic and copies ran while one was open for 58% of the time, Pallas kernels for 0%

commit v1 on v0

v1 whole, which is shorter than its diff:
```python
import jax
import jax.numpy as jnp
from jax import lax
from jax.experimental import pallas as pl
from jax.experimental.pallas import tpu as pltpu
from jax.sharding import PartitionSpec as P

LANES = 128
ROWS = 8
STEP = 8


def shifted(block, axis, distance):
    devices = range(lax.axis_size(axis))
    route = [(i - distance, i) for i in devices if i - distance in devices]
    return lax.ppermute(block, axis, route)


def scan_kernel(feat, halo, taps, decay, seg_decay, gated, fq, inclusive, ext):
    length = feat.shape[1]
    width = taps.shape[1]
    modes = decay.shape[0]
    seg = length // ROWS
    for r in range(3):
        ext[r, ROWS:, :] = feat[r].astype(jnp.float32)
        ext[r, ROWS - (width - 1) : ROWS, :] = halo[r].astype(jnp.float32)
    shape = (ROWS, LANES)
    tap = [[jnp.broadcast_to(taps[r, j : j + 1, :], shape) for j in range(width)] for r in range(3)]

    @pl.loop(0, seg // STEP)
    def _(block):
        start = block * STEP
        out = []
        for r in range(3):
            rows = [
                ext[r, pl.ds(start + i + ROWS - (width - 1), ROWS, stride=seg), :]
                for i in range(STEP + width - 1)
            ]
            out.append(
                [
                    sum(
                        (tap[r][j] * rows[i + width - 1 - j] for j in range(1, width)),
                        tap[r][0] * rows[i + width - 1],
                    )
                    for i in range(STEP)
                ]
            )
        for i in range(STEP):
            fq[start + i] = out[0][i]
            gated[start + i] = (out[1][i] * out[2][i]).astype(jnp.bfloat16).astype(jnp.float32)

    step_decay = [jnp.broadcast_to(decay[n : n + 1, :], shape) for n in range(modes)]

    def advance(block, states):
        for i in range(STEP):
            g = gated[block * STEP + i]
            states = tuple(d * s + g for d, s in zip(step_decay, states))
        return states

    states = lax.fori_loop(0, seg // STEP, advance, (jnp.zeros(shape, jnp.float32),) * modes)
    row = lax.broadcasted_iota(jnp.int32, shape, 0)
    for n in range(modes):
        value = states[n]
        factor = jnp.broadcast_to(seg_decay[n : n + 1, :], shape)
        distance = 1
        while distance < ROWS:
            value = value + jnp.where(row >= distance, factor * pltpu.roll(value, distance, 0), 0.0)
            factor = factor * factor
            distance *= 2
        inclusive[n] = value


def mix_kernel(gated, fq, inclusive, carried, rates, decay, scaled, combined, rows_out):
    seg = gated.shape[0]
    modes = decay.shape[0]
    shape = (ROWS, LANES)
    row = lax.broadcasted_iota(jnp.int32, shape, 0)
    offset = (row * seg).astype(jnp.float32)
    starts = []
    for n in range(modes):
        before = jnp.where(row == 0, 0.0, pltpu.roll(inclusive[n], 1, 0))
        starts.append(before + jnp.exp(-rates[n : n + 1, :] * offset) * carried[n : n + 1, :])
    step_decay = [jnp.broadcast_to(decay[n : n + 1, :], shape) for n in range(modes)]
    weight = [jnp.broadcast_to(scaled[n : n + 1, :], shape) for n in range(modes)]

    def advance(block, states):
        for i in range(STEP):
            t = block * STEP + i
            g = gated[t]
            states = tuple(d * s + g for d, s in zip(step_decay, states))
            terms = [w * s for w, s in zip(weight, states)]
            while len(terms) > 1:
                terms = [sum(terms[k + 1 : k + 2], terms[k]) for k in range(0, len(terms), 2)]
            rows_out[pl.ds(t, ROWS, stride=seg), :] = fq[t] * terms[0]
        return states

    lax.fori_loop(0, seg // STEP, advance, tuple(starts))
    combined[...] = rows_out[...].astype(jnp.bfloat16)


def columns(*lead):
    return pl.BlockSpec(lead + (LANES,), lambda c: (0,) * len(lead) + (c,))


def local_scan(features, halo, taps, decay, seg_decay):
    _, length, channels = features.shape
    width = taps.shape[1]
    modes = decay.shape[0]
    seg = length // ROWS
    f32 = jnp.float32
    return pl.pallas_call(
        scan_kernel,
        grid=(channels // LANES,),
        in_specs=[
            columns(3, length),
            columns(3, width - 1),
            columns(3, width),
            columns(modes),
            columns(modes),
        ],
        out_specs=[columns(seg, ROWS), columns(seg, ROWS), columns(modes, ROWS)],
        out_shape=[
            jax.ShapeDtypeStruct((seg, ROWS, channels), f32),
            jax.ShapeDtypeStruct((seg, ROWS, channels), f32),
            jax.ShapeDtypeStruct((modes, ROWS, channels), f32),
        ],
        scratch_shapes=[pltpu.VMEM((3, length + ROWS, LANES), f32)],
        compiler_params=pltpu.CompilerParams(vmem_limit_bytes=16 << 20),
        cost_estimate=pl.CostEstimate(
            flops=length * channels * (42 + 2 * modes),
            bytes_accessed=length * channels * 14,
            transcendentals=0,
        ),
        name="local_scan",
    )(features, halo, taps, decay, seg_decay)


def mix(gated, fq, inclusive, carried, rates, decay, scaled):
    seg, _, channels = gated.shape
    modes = rates.shape[0]
    length = seg * ROWS
    return pl.pallas_call(
        mix_kernel,
        grid=(channels // LANES,),
        in_specs=[columns(seg, ROWS), columns(seg, ROWS), columns(modes, ROWS)] + [columns(modes)] * 4,
        out_specs=columns(length),
        out_shape=jax.ShapeDtypeStruct((length, channels), jnp.bfloat16),
        scratch_shapes=[pltpu.VMEM((length, LANES), jnp.float32)],
        compiler_params=pltpu.CompilerParams(vmem_limit_bytes=16 << 20),
        cost_estimate=pl.CostEstimate(
            flops=length * channels * 4 * modes,
            bytes_accessed=length * channels * 10,
            transcendentals=0,
        ),
        name="mix",
    )(gated, fq, inclusive, carried, rates, decay, scaled)


def carried_state(own, rates, length):
    state = shifted(own, "ctx", 1)
    distance = 1
    while distance < lax.axis_size("ctx"):
        state = state + jnp.exp(-rates * (length * distance)) * shifted(state, "ctx", distance)
        distance *= 2
    return state


def body(features, short_filter, residues, rates, out_weight):
    length, channels = features.shape[1:]
    width = short_filter.shape[1]
    weights = lax.all_gather(out_weight, "ctx", axis=0, tiled=True)
    halo = shifted(features[:, length - (width - 1) :, :], "ctx", 1)
    scaled = (residues * jnp.sqrt(-jnp.expm1(-2.0 * rates))).T
    rates = rates.T
    decay = jnp.exp(-rates)
    gated, fq, inclusive = local_scan(
        features, halo, short_filter, decay, jnp.exp(-rates * (length // ROWS))
    )
    carried = carried_state(inclusive[:, ROWS - 1, :], rates, length)
    combined = mix(gated, fq, inclusive, carried, rates, decay, scaled)
    count, mine = lax.axis_size("mp"), lax.axis_index("mp")
    gathered = jnp.zeros((length, count * channels), jnp.bfloat16)
    for hop in range(count):
        if hop:
            ring = [(i, (i + 1) % count) for i in range(count)]
            combined = lax.ppermute(combined, "mp", ring)
        owner = lax.rem(mine + count - hop, count)
        gathered = lax.dynamic_update_slice(gathered, combined, (0, owner * channels))
    result = jnp.dot(gathered, weights, preferred_element_type=jnp.float32)
    return result.astype(jnp.bfloat16)


def solution(mesh):
    placed = (
        P(None, "ctx", "mp"),
        P(None, None, "mp"),
        P("mp", None),
        P("mp", None),
        P("ctx", "mp"),
    )
    return jax.shard_map(
        body, mesh=mesh, in_specs=placed, out_specs=P("ctx", "mp"), check_vma=False
    )
```

time: 729 us -> 197 us (0.27)
  the two profiles are of different devices: /device:TPU:0 before, /device:TPU:27 now
where the time goes in v1:
time: 197 us; the launch traced here: 196 us
  waiting for transfers between devices  95.9 us (49%)
  Pallas kernels  38.3 us (19%)
  starting transfers between devices  19.9 us (10%)
  matrix products  14.5 us (7%)
  between operations  13.5 us (7%)
  local copies, waits for them, and re-layouts  12.4 us (6%)
    ppermute x6, waiting for transfers between devices, shifted(): return lax.ppermute(block, axis, route)  53.3 us
    ppermute x1, waiting for transfers between devices, body(): combined = lax.ppermute(combined, 'mp', ring)  41.9 us
    pallas_call x1, Pallas kernels, local_scan(): pl.pallas_call(scan_kernel, grid=(channels // LANES,), in_specs=[columns(...  25.5 us
    ppermute x6, starting transfers between devices, shifted(): return lax.ppermute(block, axis, route)  16.9 us
    dot_general x1, matrix products, body(): result = jnp.dot(gathered, weights, preferred_element_type=jnp.float32)  14.5 us
    pallas_call x1, Pallas kernels, mix(): pl.pallas_call(mix_kernel, grid=(channels // LANES,), in_specs=[columns(s...  12.8 us
    dynamic_update_slice x2, local copies, waits for them, and re-layouts, body(): lax.dynamic_update_slice(gathered, combined, (0, owner * channels))  4.69 us
  transfers between devices with their start and end apart: 8, of which 7 were waited for; matrix products, arithmetic and copies ran while one was open for 5% of the time, Pallas kernels for 20%

profile of v1, /device:TPU:27, one launch (start us, length us, event | category | flops | bytes accessed | tf_op | source)
XLA Modules:
  0.0 195.7 jit_solution(7303424770898585743)
XLA Ops:
  6.5 0.0 all-gather.2.cloned.1.call-start
  6.5 0.7 all-gather.2.cloned.1.call-update
  7.3 0.9 slice.6
  8.2 3.7 %collective-permute-start = (bf16[3,6,2048]{2,1,0:T(8,128)(2,1)S(1)}, bf16[3,6,2048]{2,1,0:T(8,128)(2,1)S(1)}, u32[]{:S(2)}, u32[]{:S(2)}) collective-permute-start(bf16[3,6,2048]{2,1,0:T(8,128)(2,1)S(1)} %slice.6), channel_id=1, source_target_pairs={{0,2},{2,4},{4,6},{6,8},{8,10},{10,12},{12,14},{14,16},{16,18},{18... | collective-permute-start | bytes 221192 | tf_op jit(solution)/shard_map/ppermute | solution.py:16
  11.9 0.9 multiply_exponential_fusion
  12.8 0.7 collective-permute-done.halo
  13.5 0.0 copy-start
  13.5 2.8 %copy-done = bf16[3,512,2048]{2,1,0:T(8,128)(2,1)S(1)} copy-done((bf16[3,512,2048]{2,1,0:T(8,128)(2,1)S(1)}, bf16[3,512,2048]{2,1,0:T(8,128)(2,1)}, u32[]{:S(2)}) %copy-start) | copy-done | bytes 6291480
  16.3 0.0 copy-start.2
  16.3 0.9 copy-done.2
  17.2 0.0 copy-start.1
  17.2 0.0 copy-start.3
  17.2 25.5 %local_scan.1 = (f32[64,8,2048]{2,1,0:T(8,128)S(1)}, f32[64,8,2048]{2,1,0:T(8,128)S(1)}, f32[16,8,2048]{2,1,0:T(8,128)S(1)}) custom-call(bf16[3,512,2048]{2,1,0:T(8,128)(2,1)S(1)} %copy-done, bf16[3,6,2048]{2,1,0:T(8,128)(2,1)S(1)} %collective-permute-done.halo, f32[3,7,2048]{2,1,0:T(8,128)S(1)} %copy-done.2, f32[16,2048]{1,0:T(8,128)S(1)} %get-tuple-element.12.decay, ...), custom_call_target="tpu_custom_call" | custom-call | flops 77594624 | bytes 14680064 | tf_op jit(solution)/shard_map/local_scan/pallas_call | solution.py:111
  42.7 0.6 copy.6
  43.3 4.3 %collective-permute-start.1 = (f32[16,2048]{1,0:T(8,128)S(1)}, f32[16,2048]{1,0:T(8,128)S(1)}, u32[]{:S(2)}, u32[]{:S(2)}) collective-permute-start(f32[16,2048]{1,0:T(8,128)S(1)} %slice_bitcast_fusion), channel_id=1, source_target_pairs={{0,2},{2,4},{4,6},{6,8},{8,10},{10,12},{12,14},{14,16},{16,18},{18... | collective-permute-start | bytes 393224 | tf_op jit(solution)/shard_map/ppermute | solution.py:16
  47.7 1.9 collective-permute-done.1
  49.6 4.3 %collective-permute-start.2 = (f32[16,2048]{1,0:T(8,128)S(1)}, f32[16,2048]{1,0:T(8,128)S(1)}, u32[]{:S(2)}, u32[]{:S(2)}) collective-permute-start(f32[16,2048]{1,0:T(8,128)S(1)} %collective-permute-done.1), channel_id=1, source_target_pairs={{0,2},{2,4},{4,6},{6,8},{8,10},{10,12},{12,14},{14,16},{16,18},{18... | collective-permute-start | bytes 393224 | tf_op jit(solution)/shard_map/ppermute | solution.py:16
  54.0 6.6 %collective-permute-done.2 = f32[16,2048]{1,0:T(8,128)S(1)} collective-permute-done((f32[16,2048]{1,0:T(8,128)S(1)}, f32[16,2048]{1,0:T(8,128)S(1)}, u32[]{:S(2)}, u32[]{:S(2)}) %collective-permute-start.2) | collective-permute-done | bytes 131104 | tf_op jit(solution)/shard_map/ppermute | solution.py:16
  60.6 0.0 copy-done.1
  60.6 1.9 collective-permute-start.3
  62.5 12.5 %collective-permute-done.3 = f32[16,2048]{1,0:T(8,128)S(1)} collective-permute-done((f32[16,2048]{1,0:T(8,128)S(1)}, f32[16,2048]{1,0:T(8,128)S(1)}, u32[]{:S(2)}, u32[]{:S(2)}) %collective-permute-start.3) | collective-permute-done | bytes 131104 | tf_op jit(solution)/shard_map/ppermute | solution.py:16
  75.0 1.3 collective-permute-start.4
  76.3 13.4 %collective-permute-done.4 = f32[16,2048]{1,0:T(8,128)S(1)} collective-permute-done((f32[16,2048]{1,0:T(8,128)S(1)}, f32[16,2048]{1,0:T(8,128)S(1)}, u32[]{:S(2)}, u32[]{:S(2)}) %collective-permute-start.4) | collective-permute-done | bytes 131104 | tf_op jit(solution)/shard_map/ppermute | solution.py:16
  89.8 1.3 collective-permute-start.5
  91.1 0.0 copy-done.3
  91.1 0.1 multiply_bitcast_fusion.scaled
  91.2 18.2 %collective-permute-done.5 = f32[16,2048]{1,0:T(8,128)S(1)} collective-permute-done((f32[16,2048]{1,0:T(8,128)S(1)}, f32[16,2048]{1,0:T(8,128)S(1)}, u32[]{:S(2)}, u32[]{:S(2)}) %collective-permute-start.5) | collective-permute-done | bytes 131104 | tf_op jit(solution)/shard_map/ppermute | solution.py:16
  109.4 12.8 %mix.1 = bf16[512,2048]{1,0:T(8,128)(2,1)S(1)} custom-call(f32[64,8,2048]{2,1,0:T(8,128)S(1)} %get-tuple-element.8.gated, f32[64,8,2048]{2,1,0:T(8,128)S(1)} %get-tuple-element.9.fq, f32[16,8,2048]{2,1,0:T(8,128)S(1)} %get-tuple-element.10.inclusive, f32[16,2048]{1,0:T(8,128)S(1)} %multiply_add_fusion.carried, f32[16,2048]{1,0:T(8,128)S(1)} %bitcast.13, ...), custom_call_target="tpu_custom_call" | custom-call | flops 67108864 | bytes 10485760 | tf_op jit(solution)/shard_map/mix/pallas_call | solution.py:142
  122.3 3.0 %collective-permute-start.6 = (bf16[512,2048]{1,0:T(8,128)(2,1)S(1)}, bf16[512,2048]{1,0:T(8,128)(2,1)}, u32[]{:S(2)}, u32[]{:S(2)}) collective-permute-start(bf16[512,2048]{1,0:T(8,128)(2,1)S(1)} %mix.1), channel_id=1, source_target_pairs={{0,1},{1,0},{2,3},{3,2},{4,5},{5,4},{6,7},{7,6},{8,9},{9,8},{10,11... | collective-permute-start | bytes 6291464 | tf_op jit(solution)/shard_map/ppermute | solution.py:186
  125.3 2.5 %broadcast_in_dim.3 = bf16[512,4096]{1,0:T(8,128)(2,1)} broadcast(bf16[]{:T(256)} %constant.13.clone.1), dimensions={} | broadcast | bytes 4194306 | tf_op jit(solution)/shard_map/broadcast_in_dim | solution.py:182
  127.7 1.5 constant_dynamic-update-slice_fusion.1
  129.2 41.9 %collective-permute-done.6 = bf16[512,2048]{1,0:T(8,128)(2,1)} collective-permute-done((bf16[512,2048]{1,0:T(8,128)(2,1)S(1)}, bf16[512,2048]{1,0:T(8,128)(2,1)}, u32[]{:S(2)}, u32[]{:S(2)}) %collective-permute-start.6) | collective-permute-done | bytes 2097184 | tf_op jit(solution)/shard_map/ppermute | solution.py:186
  171.1 3.2 %constant_dynamic-update-slice_fusion = bf16[512,4096]{1,0:T(8,128)(2,1)} fusion(bf16[512,4096]{1,0:T(8,128)(2,1)} %constant_dynamic-update-slice_fusion.1, bf16[512,2048]{1,0:T(8,128)(2,1)} %collective-permute-done.6, s32[]{:T(128)S(6)} %select_n.7), kind=kLoop, calls=%fused_computation.9 | loop fusion | bytes 4194308 | tf_op jit(solution)/shard_map/dynamic_update_slice | solution.py:188
  174.3 0.0 all-gather.2.cloned.1.call-done
  174.3 14.5 %convolution_convert_fusion = bf16[512,2048]{1,0:T(8,128)(2,1)} fusion(bf16[512,4096]{1,0:T(8,128)(2,1)} %constant_dynamic-update-slice_fusion, bf16[4096,2048]{1,0:T(8,128)(2,1)} %all-gather.2.cloned.1.call-done), kind=kOutput, calls=%fused_computation | convolution fusion | flops 8590983168 | bytes 23068672 | tf_op jit(solution)/shard_map/dot_general | solution.py:189
  (5 shorter events, 0.1 us)
Async XLA Ops:
  6.5 167.8 %all-gather.2.cloned.1.call-start = ((), (), s32[]{:S(2)}) async-start(), calls=%async_computation | async-start | bytes 17825792 | tf_op jit(solution)/shard_map/all_gather | solution.py:171
  8.2 5.3 %collective-permute-start = (bf16[3,6,2048]{2,1,0:T(8,128)(2,1)S(1)}, bf16[3,6,2048]{2,1,0:T(8,128)(2,1)S(1)}, u32[]{:S(2)}, u32[]{:S(2)}) collective-permute-start(bf16[3,6,2048]{2,1,0:T(8,128)(2,1)S(1)} %slice.6), channel_id=1, source_target_pairs={{0,2},{2,4},{4,6},{6,8},{8,10},{10,12},{12,14},{14,16},{16,18},{18... | collective-permute-start | bytes 221192 | tf_op jit(solution)/shard_map/ppermute | solution.py:16
  13.5 2.8 %copy-start = (bf16[3,512,2048]{2,1,0:T(8,128)(2,1)S(1)}, bf16[3,512,2048]{2,1,0:T(8,128)(2,1)}, u32[]{:S(2)}) copy-start(bf16[3,512,2048]{2,1,0:T(8,128)(2,1)} %feat.1) | copy-start | bytes 18874372
  16.3 0.9 copy-start.2
  17.2 43.3 %copy-start.1 = (f32[2048,16]{0,1:T(8,128)S(1)}, f32[2048,16]{0,1:T(8,128)}, u32[]{:S(2)}) copy-start(f32[2048,16]{0,1:T(8,128)} %param.8) | copy-start | bytes 393220
  17.2 73.8 %copy-start.3 = (f32[2048,16]{0,1:T(8,128)S(1)}, f32[2048,16]{0,1:T(8,128)}, u32[]{:S(2)}) copy-start(f32[2048,16]{0,1:T(8,128)} %param.7) | copy-start | bytes 393220
  43.3 6.3 %collective-permute-start.1 = (f32[16,2048]{1,0:T(8,128)S(1)}, f32[16,2048]{1,0:T(8,128)S(1)}, u32[]{:S(2)}, u32[]{:S(2)}) collective-permute-start(f32[16,2048]{1,0:T(8,128)S(1)} %slice_bitcast_fusion), channel_id=1, source_target_pairs={{0,2},{2,4},{4,6},{6,8},{8,10},{10,12},{12,14},{14,16},{16,18},{18... | collective-permute-start | bytes 393224 | tf_op jit(solution)/shard_map/ppermute | solution.py:16
  49.6 10.9 %collective-permute-start.2 = (f32[16,2048]{1,0:T(8,128)S(1)}, f32[16,2048]{1,0:T(8,128)S(1)}, u32[]{:S(2)}, u32[]{:S(2)}) collective-permute-start(f32[16,2048]{1,0:T(8,128)S(1)} %collective-permute-done.1), channel_id=1, source_target_pairs={{0,2},{2,4},{4,6},{6,8},{8,10},{10,12},{12,14},{14,16},{16,18},{18... | collective-permute-start | bytes 393224 | tf_op jit(solution)/shard_map/ppermute | solution.py:16
  60.6 14.4 %collective-permute-start.3 = (f32[16,2048]{1,0:T(8,128)S(1)}, f32[16,2048]{1,0:T(8,128)S(1)}, u32[]{:S(2)}, u32[]{:S(2)}) collective-permute-start(f32[16,2048]{1,0:T(8,128)S(1)} %multiply_add_fusion.3), channel_id=1, source_target_pairs={{0,4},{2,6},{4,8},{6,10},{8,12},{10,14},{12,16},{14,18},{16,20},{1... | collective-permute-start | bytes 393224 | tf_op jit(solution)/shard_map/ppermute | solution.py:16
  75.0 14.7 %collective-permute-start.4 = (f32[16,2048]{1,0:T(8,128)S(1)}, f32[16,2048]{1,0:T(8,128)S(1)}, u32[]{:S(2)}, u32[]{:S(2)}) collective-permute-start(f32[16,2048]{1,0:T(8,128)S(1)} %multiply_add_fusion.2), channel_id=1, source_target_pairs={{0,8},{2,10},{4,12},{6,14},{8,16},{10,18},{12,20},{14,22},{16,24},... | collective-permute-start | bytes 393224 | tf_op jit(solution)/shard_map/ppermute | solution.py:16
  89.8 19.6 %collective-permute-start.5 = (f32[16,2048]{1,0:T(8,128)S(1)}, f32[16,2048]{1,0:T(8,128)S(1)}, u32[]{:S(2)}, u32[]{:S(2)}) collective-permute-start(f32[16,2048]{1,0:T(8,128)S(1)} %multiply_add_fusion.1), channel_id=1, source_target_pairs={{0,16},{2,18},{4,20},{6,22},{8,24},{10,26},{12,28},{14,30},{1,17},... | collective-permute-start | bytes 393224 | tf_op jit(solution)/shard_map/ppermute | solution.py:16
  122.3 48.8 %collective-permute-start.6 = (bf16[512,2048]{1,0:T(8,128)(2,1)S(1)}, bf16[512,2048]{1,0:T(8,128)(2,1)}, u32[]{:S(2)}, u32[]{:S(2)}) collective-permute-start(bf16[512,2048]{1,0:T(8,128)(2,1)S(1)} %mix.1), channel_id=1, source_target_pairs={{0,1},{1,0},{2,3},{3,2},{4,5},{5,4},{6,7},{7,6},{8,9},{9,8},{10,11... | collective-permute-start | bytes 6291464 | tf_op jit(solution)/shard_map/ppermute | solution.py:186
Sparse Core Ops, SparseCore 0:
  9.5 133.1 all-gather.1

commit v2 on v0

v2 whole, which is shorter than its diff:
```python
import jax
import jax.numpy as jnp
from jax import lax
from jax.experimental import pallas as pl
from jax.experimental.pallas import tpu as pltpu
from jax.sharding import PartitionSpec as P

LANES = 128
ROWS = 8
STEP = 8
HALO = 16
F32 = jnp.float32
MESH = pl.DeviceIdType.MESH


def mixer_kernel(n, m, feat, taps, decay, seg_decay, rates, scaled, own_weight, out,
                 halo, ext, gated, fq, inclusive, states, arrived, weight, combined, total,
                 w_send, w_recv, s_send, s_recv, x_send, x_recv, h_send, h_recv, local_sem):
    length, channels = feat.shape[1:]
    width = taps.shape[1]
    modes = decay.shape[0]
    depth, wide = own_weight.shape
    seg = length // ROWS
    blocks = channels // LANES
    chips = n // 2
    side = 2 if chips % 2 == 0 else 1
    line = chips // side
    me, mine = lax.axis_index("ctx"), lax.axis_index("mp")
    core = lax.rem(me, 2)
    chip = lax.div(me, 2)
    b = lax.rem(chip, side)
    a = lax.div(chip, side)
    partner = me + 1 - 2 * core
    across = me + 2 * (1 - 2 * b)
    jump = 2 * side
    distances = [1 << k for k in range(n.bit_length()) if (1 << k) < n]

    barrier = pltpu.get_barrier_semaphore()
    for d in distances:
        for sign in (1, -1):
            other = me + sign * d

            @pl.when((other >= 0) & (other < n))
            def _():
                pl.semaphore_signal(barrier, inc=1, device_id={"ctx": other}, device_id_type=MESH)

    for k in range(1, m):
        pl.semaphore_signal(
            barrier, inc=1, device_id={"mp": lax.rem(mine + k, m)}, device_id_type=MESH
        )
    peers = m - 1
    for d in distances:
        peers = peers + (me >= d).astype(jnp.int32) + (me + d < n).astype(jnp.int32)
    pl.semaphore_wait(barrier, peers)

    def slot(s):
        return weight.at[pl.ds(pl.multiple_of(s * depth, depth), depth), :]

    def push(kind, s, to, source=None):
        return pltpu.make_async_remote_copy(
            src_ref=slot(s) if source is None else source,
            dst_ref=slot(s),
            send_sem=w_send.at[kind, s],
            recv_sem=w_recv.at[s],
            device_id={"ctx": to},
            device_id_type=MESH,
        )

    def halo_copy():
        return pltpu.make_async_remote_copy(
            src_ref=feat.at[:, length - HALO :, :],
            dst_ref=halo,
            send_sem=h_send,
            recv_sem=h_recv,
            device_id={"ctx": lax.rem(me + 1, n)},
            device_id_type=MESH,
        )

    up, down = a < line - 1, a > 0

    @pl.when(me < n - 1)
    def _():
        halo_copy().start()

    @pl.when(up)
    def _():
        push(0, me, me + jump, own_weight).start()

    @pl.when(down)
    def _():
        push(1, me, me - jump, own_weight).start()

    if side == 2:
        push(2, me, across, own_weight).start()
    push(3, me, partner, own_weight).start()
    keep = pltpu.make_async_copy(own_weight, slot(me), local_sem)
    keep.start()

    @pl.when(me > 0)
    def _():
        halo_copy().wait_recv()

    @pl.when(me == 0)
    def _():
        halo[...] = jnp.zeros_like(halo)

    shape = (ROWS, LANES)
    row = lax.broadcasted_iota(jnp.int32, shape, 0)

    @pl.loop(0, blocks)
    def _(c):
        cols = pl.ds(pl.multiple_of(c * LANES, LANES), LANES)
        for r in range(3):
            ext[r, ROWS:, :] = feat[r, :, cols].astype(F32)
            ext[r, :ROWS, :] = halo[r, :, cols].astype(F32)[HALO - ROWS :, :]
        tap = [
            [jnp.broadcast_to(taps[r, j : j + 1, cols], shape) for j in range(width)]
            for r in range(3)
        ]

        @pl.loop(0, seg // STEP)
        def _(block):
            start = block * STEP
            made = []
            for r in range(3):
                rows = [
                    ext[r, pl.ds(start + i + ROWS - (width - 1), ROWS, stride=seg), :]
                    for i in range(STEP + width - 1)
                ]
                made.append(
                    [
                        sum(
                            (tap[r][j] * rows[i + width - 1 - j] for j in range(1, width)),
                            tap[r][0] * rows[i + width - 1],
                        )
                        for i in range(STEP)
                    ]
                )
            for i in range(STEP):
                at = c * seg + start + i
                fq[at] = made[0][i]
                gated[at] = (made[1][i] * made[2][i]).astype(jnp.bfloat16).astype(F32)

        step_decay = [jnp.broadcast_to(decay[k : k + 1, cols], shape) for k in range(modes)]

        def advance(block, modal):
            for i in range(STEP):
                g = gated[c * seg + block * STEP + i]
                modal = tuple(d * s + g for d, s in zip(step_decay, modal))
            return modal

        modal = lax.fori_loop(0, seg // STEP, advance, (jnp.zeros(shape, F32),) * modes)
        for k in range(modes):
            value = modal[k]
            factor = jnp.broadcast_to(seg_decay[k : k + 1, cols], shape)
            distance = 1
            while distance < ROWS:
                earlier = pltpu.roll(value, distance, 0)
                value = value + jnp.where(row >= distance, factor * earlier, 0.0)
                factor = factor * factor
                distance *= 2
            inclusive[c * modes + k] = value
            states[0, k : k + 1, cols] = value[ROWS - 1 :, :]

    hops = [1] + distances
    for level, d in enumerate(hops):
        def hop_copy(level=level, d=d):
            return pltpu.make_async_remote_copy(
                src_ref=states.at[level],
                dst_ref=arrived.at[level],
                send_sem=s_send.at[level],
                recv_sem=s_recv.at[level],
                device_id={"ctx": lax.rem(me + d, n)},
                device_id_type=MESH,
            )

        @pl.when(me + d < n)
        def _():
            hop_copy().start()

        @pl.when(me >= d)
        def _():
            hop_copy().wait_recv()
            if level == 0:
                states[1] = arrived[0]
            else:
                states[level + 1] = states[level] + jnp.exp(rates[...] * (-1.0 * length * d)) * arrived[level]

        @pl.when(me < d)
        def _():
            states[level + 1] = jnp.zeros_like(states[1]) if level == 0 else states[level]

    carried = len(hops)

    def take(s):
        push(3, s, partner).wait_recv()

    def serve_line(k):
        @pl.when(a >= k)
        def _():
            s = me - k * jump
            take(s)
            if side == 2:
                push(2, s, across).start()

            @pl.when(up)
            def _():
                push(0, s, me + jump).start()

            push(3, s, partner).start()

        @pl.when(a + k < line)
        def _():
            s = me + k * jump
            take(s)
            if side == 2:
                push(2, s, across).start()

            @pl.when(down)
            def _():
                push(1, s, me - jump).start()

            push(3, s, partner).start()

    def serve_side(k):
        if side == 2:
            for sign in (1, -1) if k else (1,):
                @pl.when((a + sign * k >= 0) & (a + sign * k < line))
                def _():
                    s = across + sign * k * jump
                    take(s)
                    push(3, s, partner).start()

    if line > 1:
        serve_line(1)
    serve_side(0)

    parts = x_recv.shape[1]
    part = channels // parts

    def swap(k, p):
        where = combined.at[mine, :, pl.ds(pl.multiple_of(p * part, part), part)]
        return pltpu.make_async_remote_copy(
            src_ref=where,
            dst_ref=where,
            send_sem=x_send.at[k, p],
            recv_sem=x_recv.at[mine, p],
            device_id={"mp": lax.rem(mine + k, m)},
            device_id_type=MESH,
        )

    offset = (row * seg).astype(F32)

    @pl.loop(0, parts)
    def _(p):
        @pl.loop(0, blocks // parts)
        def _(q):
            c = p * (blocks // parts) + q
            cols = pl.ds(pl.multiple_of(c * LANES, LANES), LANES)
            starts = []
            for k in range(modes):
                before = jnp.where(row == 0, 0.0, pltpu.roll(inclusive[c * modes + k], 1, 0))
                fade = jnp.exp(-rates[k : k + 1, cols] * offset)
                starts.append(before + fade * states[carried, k : k + 1, cols])
            step_decay = [jnp.broadcast_to(decay[k : k + 1, cols], shape) for k in range(modes)]
            gain = [jnp.broadcast_to(scaled[k : k + 1, cols], shape) for k in range(modes)]

            def advance(block, modal):
                for i in range(STEP):
                    t = block * STEP + i
                    g = gated[c * seg + t]
                    modal = tuple(d * s + g for d, s in zip(step_decay, modal))
                    terms = [w * s for w, s in zip(gain, modal)]
                    while len(terms) > 1:
                        terms = [sum(terms[k + 1 : k + 2], terms[k]) for k in range(0, len(terms), 2)]
                    ext[0, pl.ds(t, ROWS, stride=seg), :] = fq[c * seg + t] * terms[0]
                return modal

            lax.fori_loop(0, seg // STEP, advance, tuple(starts))
            combined[mine, :, cols] = ext[0, :length, :].astype(jnp.bfloat16)

        for k in range(1, m):
            swap(k, p).start()

    for k in range(2, line):
        serve_line(k)
        serve_side(k - 1)

    for k in range(max(line - 1, 1), line):
        serve_side(k)

    keep.wait()

    tile = 256 if wide % 256 == 0 else wide
    per_group = chips // m

    def multiply(group, first):
        def one(k, h):
            aa = lax.div(group * per_group, side) + k
            bb = lax.rem(b + h, side)
            which = aa * side + bb
            take(which * 2 + 1 - core)
            rows = pl.ds(pl.multiple_of(which * 2 * depth, 2 * depth), 2 * depth)
            take_cols = pl.ds(
                pl.multiple_of((which - group * per_group) * 2 * depth, 2 * depth), 2 * depth
            )

            @pl.loop(0, wide // tile)
            def _(j):
                cols = pl.ds(pl.multiple_of(j * tile, tile), tile)
                product = jnp.dot(
                    combined[group, :, take_cols], weight[rows, cols], preferred_element_type=F32
                )
                if first and h == 0:
                    @pl.when(k == 0)
                    def _():
                        total[:, cols] = product

                    @pl.when(k > 0)
                    def _():
                        total[:, cols] += product
                else:
                    total[:, cols] += product

        for h in range(side):
            @pl.loop(0, per_group // side)
            def _(k, h=h):
                one(k, h)

    multiply(mine, True)
    for k in range(1, m):
        group = lax.rem(mine + k, m)
        for p in range(parts):
            where = combined.at[group, :, p * part : (p + 1) * part]
            pltpu.make_async_remote_copy(
                src_ref=where,
                dst_ref=where,
                send_sem=x_send.at[k, p],
                recv_sem=x_recv.at[group, p],
                device_id={"mp": group},
                device_id_type=MESH,
            ).wait_recv()
        multiply(group, False)

    out[...] = total[...].astype(out.dtype)

    @pl.when(me < n - 1)
    def _():
        halo_copy().wait_send()

    for level, d in enumerate(hops):
        @pl.when(me + d < n)
        def _(level=level, d=d):
            pltpu.make_async_remote_copy(
                src_ref=states.at[level],
                dst_ref=arrived.at[level],
                send_sem=s_send.at[level],
                recv_sem=s_recv.at[level],
                device_id={"ctx": lax.rem(me + d, n)},
                device_id_type=MESH,
            ).wait_send()

    for k in range(1, m):
        for p in range(parts):
            swap(k, p).wait_send()

    @pl.loop(0, line)
    def _(aa):
        s = (aa * side + b) * 2 + core

        @pl.when(up & (aa <= a))
        def _():
            push(0, s, me + jump).wait_send()

        @pl.when(down & (aa >= a))
        def _():
            push(1, s, me - jump).wait_send()

        if side == 2:
            push(2, s, across).wait_send()

    @pl.loop(0, chips)
    def _(which):
        push(3, which * 2 + core, partner).wait_send()


def mixer(features, taps, decay, seg_decay, rates, scaled, own_weight):
    n, m = lax.axis_size("ctx"), lax.axis_size("mp")
    length, channels = features.shape[1:]
    modes = rates.shape[0]
    depth, wide = own_weight.shape
    blocks = channels // LANES
    seg = length // ROWS
    levels = 1 + len([k for k in range(n.bit_length()) if (1 << k) < n])
    parts = 4 if blocks % 4 == 0 else 1
    dma = pltpu.SemaphoreType.DMA
    whole = pl.BlockSpec(memory_space=pltpu.VMEM)
    return pl.pallas_call(
        lambda *refs: mixer_kernel(n, m, *refs),
        out_shape=jax.ShapeDtypeStruct((length, wide), jnp.bfloat16),
        in_specs=[whole] * 7,
        out_specs=whole,
        scratch_shapes=[
            pltpu.VMEM((3, HALO, channels), jnp.bfloat16),
            pltpu.VMEM((3, length + ROWS, LANES), F32),
            pltpu.VMEM((blocks * seg, ROWS, LANES), F32),
            pltpu.VMEM((blocks * seg, ROWS, LANES), F32),
            pltpu.VMEM((blocks * modes, ROWS, LANES), F32),
            pltpu.VMEM((levels + 1, modes, channels), F32),
            pltpu.VMEM((levels, modes, channels), F32),
            pltpu.VMEM((n * depth, wide), jnp.bfloat16),
            pltpu.VMEM((m, length, channels), jnp.bfloat16),
            pltpu.VMEM((length, wide), F32),
            dma((4, n)),
            dma((n,)),
            dma((levels,)),
            dma((levels,)),
            dma((m, parts)),
            dma((m, parts)),
            dma,
            dma,
            dma,
        ],
        compiler_params=pltpu.CompilerParams(
            collective_id=0, has_side_effects=True, vmem_limit_bytes=58 << 20
        ),
        name="mixer",
    )(features, taps, decay, seg_decay, rates, scaled, own_weight)


def body(features, short_filter, residues, rates, out_weight):
    length = features.shape[1]
    scaled = (residues * jnp.sqrt(-jnp.expm1(-2.0 * rates))).T
    rates = rates.T
    decay = jnp.exp(-rates)
    seg_decay = jnp.exp(-rates * (length // ROWS))
    return mixer(features, short_filter, decay, seg_decay, rates, scaled, out_weight)


def solution(mesh):
    placed = (
        P(None, "ctx", "mp"),
        P(None, None, "mp"),
        P("mp", None),
        P("mp", None),
        P("ctx", "mp"),
    )
    return jax.shard_map(
        body, mesh=mesh, in_specs=placed, out_specs=P("ctx", "mp"), check_vma=False
    )
```

time: 729 us -> 150 us (0.21)
  the two profiles are of different devices: /device:TPU:0 before, /device:TPU:27 now
where the time goes in v2:
time: 150 us; the launch traced here: 148 us
  Pallas kernels  141 us (94%)
  other arithmetic  3.36 us (2%)
  local copies, waits for them, and re-layouts  3.16 us (2%)
    pallas_call x1, Pallas kernels, mixer(): pl.pallas_call(lambda *refs: mixer_kernel(n, m, *refs), out_shape=jax.Sha...  141 us
    unnamed x1, local copies, waits for them, and re-layouts  3.16 us

profile of v2, /device:TPU:27, one launch (start us, length us, event | category | flops | bytes accessed | tf_op | source)
XLA Modules:
  0.0 147.6 jit_solution(1054744333027378845)
XLA Ops:
  0.0 1.7 %multiply_bitcast_fusion.refs_5_ = f32[16,2048]{1,0:T(8,128)} fusion(f32[2048,16]{0,1:T(8,128)} %param.7, f32[2048,16]{0,1:T(8,128)} %param.8), kind=kLoop, calls=%fused_computation | loop fusion | flops 98304 | bytes 393216 | tf_op jit(solution)/shard_map/transpose | solution.py:433
  1.7 1.7 %multiply_exponential_fusion = (f32[16,2048]{1,0:T(8,128)}, f32[16,2048]{1,0:T(8,128)}) fusion(f32[2048,16]{0,1:T(8,128)} %param.8), kind=kLoop, calls=%fused_computation.1 | loop fusion | flops 65536 | bytes 393216 | tf_op jit(solution)/shard_map/exp | solution.py:436
  3.4 141.0 %mixer.1 = bf16[512,2048]{1,0:T(8,128)(2,1)} custom-call(bf16[3,512,2048]{2,1,0:T(8,128)(2,1)} %refs_0_.1, f32[3,7,2048]{2,1,0:T(8,128)} %refs_1_.1, f32[16,2048]{1,0:T(8,128)} %get-tuple-element.6.refs_2_, f32[16,2048]{1,0:T(8,128)} %get-tuple-element.5.refs_3_, f32[16,2048]{1,0:T(8,128)} %bitcast.5, f32[16,2048]{1,0:T(8,128)} %multiply_bitcast_fusion.refs_5_, ...), custom_call_target="tpu_custom_call" | custom-call | tf_op jit(solution)/shard_map/mixer/pallas_call | solution.py:398
  144.4 3.2 %copy.7 = bf16[512,2048]{1,0:T(8,128)(2,1)} copy(bf16[512,2048]{1,0:T(8,128)(2,1)} %mixer.1) | data formatting | bytes 4194304

commit v3 on v2

--- a/solution.py
+++ b/solution.py
@@ -284,50 +284,12 @@
 
     for k in range(2, line):
         serve_line(k)
-        serve_side(k - 1)
-
-    for k in range(max(line - 1, 1), line):
-        serve_side(k)
-
+        if k == 2:
+            serve_side(1)
+
+    if line == 2:
+        serve_side(1)
     keep.wait()
-
-    tile = 256 if wide % 256 == 0 else wide
-    per_group = chips // m
-
-    def multiply(group, first):
-        def one(k, h):
-            aa = lax.div(group * per_group, side) + k
-            bb = lax.rem(b + h, side)
-            which = aa * side + bb
-            take(which * 2 + 1 - core)
-            rows = pl.ds(pl.multiple_of(which * 2 * depth, 2 * depth), 2 * depth)
-            take_cols = pl.ds(
-                pl.multiple_of((which - group * per_group) * 2 * depth, 2 * depth), 2 * depth
-            )
-
-            @pl.loop(0, wide // tile)
-            def _(j):
-                cols = pl.ds(pl.multiple_of(j * tile, tile), tile)
-                product = jnp.dot(
-                    combined[group, :, take_cols], weight[rows, cols], preferred_element_type=F32
-                )
-                if first and h == 0:
-                    @pl.when(k == 0)
-                    def _():
-                        total[:, cols] = product
-
-                    @pl.when(k > 0)
-                    def _():
-                        total[:, cols] += product
-                else:
-                    total[:, cols] += product
-
-        for h in range(side):
-            @pl.loop(0, per_group // side)
-            def _(k, h=h):
-                one(k, h)
-
-    multiply(mine, True)
     for k in range(1, m):
         group = lax.rem(mine + k, m)
         for p in range(parts):
@@ -340,7 +302,41 @@
                 device_id={"mp": group},
                 device_id_type=MESH,
             ).wait_recv()
-        multiply(group, False)
+
+    tile = 256 if wide % 256 == 0 else wide
+    per_group = chips // m
+
+    def multiply(aa, bb, first=False):
+        which = aa * side + bb
+        take(which * 2 + 1 - core)
+        group = lax.div(which, per_group)
+        rows = pl.ds(pl.multiple_of(which * 2 * depth, 2 * depth), 2 * depth)
+        inner = pl.ds(
+            pl.multiple_of((which - group * per_group) * 2 * depth, 2 * depth), 2 * depth
+        )
+
+        @pl.loop(0, wide // tile)
+        def _(j):
+            cols = pl.ds(pl.multiple_of(j * tile, tile), tile)
+            product = jnp.dot(
+                combined[group, :, inner], weight[rows, cols], preferred_element_type=F32
+            )
+            total[:, cols] = product if first else total[:, cols] + product
+
+    def multiply_at(k, bb):
+        for sign in (1, -1) if k else (1,):
+            @pl.when((a + sign * k >= 0) & (a + sign * k < line))
+            def _():
+                multiply(a + sign * k, bb)
+
+    multiply(a, b, first=True)
+    for k in range(1, line):
+        multiply_at(k, b)
+    if side == 2:
+        for k in range(line):
+            if k >= 2:
+                serve_side(k)
+            multiply_at(k, 1 - b)
 
     out[...] = total[...].astype(out.dtype)
 

time: 150 us -> 134 us (0.89); the launches traced: 148 us -> 134 us
  Pallas kernels: 141 us -> 128 us
    pallas_call x1, Pallas kernels: 141 us -> 128 us  [mixer(): pl.pallas_call(lambda *refs: mixer_kernel(n, m, *refs), out_shape=jax.Sha...]
where the time goes in v3:
time: 134 us
  Pallas kernels  128 us (96%)
  other arithmetic  3.36 us (3%)
  local copies, waits for them, and re-layouts  3.16 us (2%)
    pallas_call x1, Pallas kernels, mixer(): pl.pallas_call(lambda *refs: mixer_kernel(n, m, *refs), out_shape=jax.Sha...  128 us
    unnamed x1, local copies, waits for them, and re-layouts  3.16 us

profile of v3, /device:TPU:27, one launch (start us, length us, event | category | flops | bytes accessed | tf_op | source)
XLA Modules:
  0.0 134.1 jit_solution(623512046651069465)
XLA Ops:
  0.0 1.7 %multiply_bitcast_fusion.refs_5_ = f32[16,2048]{1,0:T(8,128)} fusion(f32[2048,16]{0,1:T(8,128)} %param.7, f32[2048,16]{0,1:T(8,128)} %param.8), kind=kLoop, calls=%fused_computation | loop fusion | flops 98304 | bytes 393216 | tf_op jit(solution)/shard_map/transpose | solution.py:429
  1.7 1.7 %multiply_exponential_fusion = (f32[16,2048]{1,0:T(8,128)}, f32[16,2048]{1,0:T(8,128)}) fusion(f32[2048,16]{0,1:T(8,128)} %param.8), kind=kLoop, calls=%fused_computation.1 | loop fusion | flops 65536 | bytes 393216 | tf_op jit(solution)/shard_map/exp | solution.py:432
  3.4 127.5 %mixer.1 = bf16[512,2048]{1,0:T(8,128)(2,1)} custom-call(bf16[3,512,2048]{2,1,0:T(8,128)(2,1)} %refs_0_.1, f32[3,7,2048]{2,1,0:T(8,128)} %refs_1_.1, f32[16,2048]{1,0:T(8,128)} %get-tuple-element.6.refs_2_, f32[16,2048]{1,0:T(8,128)} %get-tuple-element.5.refs_3_, f32[16,2048]{1,0:T(8,128)} %bitcast.5, f32[16,2048]{1,0:T(8,128)} %multiply_bitcast_fusion.refs_5_, ...), custom_call_target="tpu_custom_call" | custom-call | tf_op jit(solution)/shard_map/mixer/pallas_call | solution.py:394
  130.9 3.2 %copy.7 = bf16[512,2048]{1,0:T(8,128)(2,1)} copy(bf16[512,2048]{1,0:T(8,128)(2,1)} %mixer.1) | data formatting | bytes 4194304
